TPU v7x, 32 devices: a whole 2x2x4 slice. The times are simulated.
32 devices in a mesh: row: 4 (over y, x), col: 4 (over z), depth: 2 (over core).
Axes of the slice: x: 2, y: 2, z: 4, core: 2. Of those that a mesh axis runs over, the one named last changes fastest.
Arguments:
- left_outer: bfloat16 [4, 8, 2048, 128], P('row', 'depth', 'col'), may hold values from -6 to 6
- left_inner: bfloat16 [4, 8, 2048, 128], P('row', 'depth', 'col'), may hold values from -0.125 to 0.125
- right_outer: bfloat16 [4, 8, 2048, 128], P('col', 'depth', 'row'), may hold values from -6 to 6
- right_inner: bfloat16 [4, 8, 2048, 128], P('col', 'depth', 'row'), may hold values from -0.125 to 0.125
- range_test: bfloat16 [4, 2048, 128], P('col', 'row'), may hold values from -0.125 to 0.125
- corange_test: bfloat16 [4, 2048, 256], P('row', 'col'), may hold values from -0.125 to 0.125
- product_mask: int32 [4, 4, 8], P('row', 'col', 'depth'), may hold values 0 or 1
Outputs:
- range_factor: float32 [4, 4, 2048, 128], P('row', 'col', 'depth')
- corange_factor: float32 [4, 4, 2048, 128], P('row', 'col', 'depth')
All inputs are finite; a program needn't handle non-finite values. No bound on the sum of `product_mask` on one device may be relied on, other than what follows from the above.
Results may differ from a plain program's by a relative error of at most 0.0093.
Values may be sent and summed in bfloat16 or wider, within the bound.
A program may use at most 64 MiB of HBM per device.

v0:
```python
import jax
import jax.numpy as jnp
from jax import lax
from jax.sharding import PartitionSpec as P


def body(left_outer, left_inner, right_outer, right_inner, range_test, corange_test, product_mask):
    flt = jnp.float32
    half = jnp.bfloat16
    highest = lax.Precision.HIGHEST
    depth_count = lax.axis_size("depth")
    inner_total = left_outer.shape[1] * depth_count
    scale = inner_total ** (-0.5)
    rank_width = left_outer.shape[3]
    outer_right, inner_right, test_range = (
        lax.all_gather(right_outer, "row", axis=2, tiled=True),
        lax.all_gather(right_inner, "row", axis=2, tiled=True),
        lax.all_gather(range_test, "row", axis=1, tiled=True),
    )
    probe = jnp.einsum(
        "kbr,bs->krs", outer_right[0], test_range[0], preferred_element_type=flt
    ).astype(half)
    outer_left, inner_left, test_corange = (
        lax.all_gather(left_outer, "col", axis=2, tiled=True),
        lax.all_gather(left_inner, "col", axis=2, tiled=True),
        lax.all_gather(corange_test, "col", axis=1, tiled=True),
    )
    basis_left = outer_left[0]
    basis_right = outer_right[0]
    test_full = test_corange[0]
    test_left = jnp.einsum("bs,kbr->ksr", test_full, basis_left, preferred_element_type=flt).astype(
        half
    )
    cross = jnp.einsum(
        "kbr,kbs->krs", inner_left[0], inner_right[0], preferred_element_type=flt
    ).astype(half)
    weight = (product_mask[0, 0].astype(flt) * scale)[:, None, None]
    core_right = (
        jnp.einsum("krs,kst->krt", cross, probe, preferred_element_type=flt) * weight
    ).astype(half)
    core_left = (
        jnp.einsum("kar,krs->kas", test_left, cross, preferred_element_type=flt) * weight
    ).astype(half)
    range_part = jnp.einsum("kbr,krs->bs", basis_left, core_right, preferred_element_type=flt)
    corange_part = jnp.einsum("kbs,kas->ba", basis_right, core_left, preferred_element_type=flt)
    core_part = jnp.dot(test_full.astype(flt).T, range_part, precision=highest)
    core = lax.psum(core_part, "depth")
    range_rows, corange_rows = (
        lax.psum_scatter(range_part, "depth", scatter_dimension=0, tiled=True),
        lax.psum_scatter(corange_part, "depth", scatter_dimension=0, tiled=True),
    )
    gram = jnp.dot(core.T, core, precision=highest)
    ridge = 0.05 * jnp.trace(gram) / rank_width + 1e-05
    gram = gram + ridge * jnp.eye(rank_width, dtype=flt)
    lower = jnp.linalg.cholesky(gram)
    projected = jnp.dot(corange_rows, core, precision=highest)
    solved = jax.scipy.linalg.cho_solve((lower, True), projected.T).T * rank_width**0.5
    return (range_rows[None, None], solved[None, None])


def solution(mesh):
    return jax.shard_map(
        body,
        mesh=mesh,
        in_specs=(
            P("row", "depth", "col", None),
            P("row", "depth", "col", None),
            P("col", "depth", "row", None),
            P("col", "depth", "row", None),
            P("col", "row", None),
            P("row", "col", None),
            P("row", "col", "depth"),
        ),
        out_specs=(P("row", "col", "depth", None), P("row", "col", "depth", None)),
        check_vma=False,
    )
```

profile of v0, /device:TPU:0, one launch (start us, length us, event | category | flops | bytes accessed | tf_op | source)
XLA Modules:
  0.0 265.8 jit_solution(3278527912864598622)
XLA Ops:
  7.2 0.0 copy-start.2
  7.2 0.0 copy-start.3
  7.2 0.0 all-gather.6.cloned.1.call-start
  7.2 2.1 copy.9
  9.3 0.0 all-gather.6.cloned.1.call-update
  9.3 0.0 all-gather.8.cloned.1.call-start
  9.4 0.7 all-gather.8.cloned.1.call-update
  10.1 0.0 all-gather.10.cloned.1.call-start
  10.1 0.7 all-gather.10.cloned.1.call-update
  10.8 0.0 all-gather.12.cloned.1.call-start
  10.8 0.5 all-gather.12.cloned.1.call-update
  11.4 0.0 all-gather.14.cloned.1.call-start
  11.4 0.5 all-gather.14.cloned.1.call-update
  12.0 0.0 all-reduce.2.cloned.1.call-start
  12.0 0.0 copy-done.2
  12.0 11.5 %all_gather.21 = bf16[1,2048,128]{2,1,0:T(8,128)(2,1)S(1)} all-gather(bf16[1,512,128]{2,1,0:T(8,128)(2,1)S(1)} %copy-done.2), channel_id=1, replica_groups=mesh['row'=4,'col'=4,'depth'=2] {'row'}, dimensions={1}, use_global_device_ids=true | all-gather | bytes 655360 | tf_op jit(solution)/shard_map/all_gather | solution.py:18
  23.5 0.0 copy-done.3
  23.6 35.0 %all-gather.6.cloned.1.call-done = bf16[1,4,2048,128]{2,3,1,0:T(8,128)(2,1)} async-done(((bf16[1,4,512,128]{2,3,1,0:T(8,128)(2,1)}), bf16[1,4,2048,128]{2,3,1,0:T(8,128)(2,1)}) %all-gather.6.cloned.1.call-update) | async-done | bytes 2097168 | tf_op jit(solution)/shard_map/all_gather | solution.py:25
  58.5 35.9 %all-gather.8.cloned.1.call-done = bf16[1,4,2048,128]{3,2,1,0:T(8,128)(2,1)} async-done(((bf16[1,4,512,128]{3,2,1,0:T(8,128)(2,1)}), bf16[1,4,2048,128]{3,2,1,0:T(8,128)(2,1)}) %all-gather.8.cloned.1.call-update) | async-done | bytes 2097168 | tf_op jit(solution)/shard_map/all_gather | solution.py:17
  94.4 2.9 %fusion.19 = bf16[4,128,128]{2,1,0:T(8,128)(2,1)S(1)} fusion(bf16[1,4,2048,128]{3,2,1,0:T(8,128)(2,1)} %all-gather.8.cloned.1.call-done, bf16[1,4,2048,128]{2,3,1,0:T(8,128)(2,1)} %all-gather.6.cloned.1.call-done), kind=kOutput, calls=%fused_computation.19 | convolution fusion | flops 268500992 | bytes 4325376 | tf_op jit(solution)/shard_map/kbr,kbs->krs/dot_general | solution.py:34
  97.3 34.1 %all-gather.10.cloned.1.call-done = bf16[1,4,2048,128]{3,2,1,0:T(8,128)(2,1)} async-done(((bf16[1,4,512,128]{3,2,1,0:T(8,128)(2,1)}), bf16[1,4,2048,128]{3,2,1,0:T(8,128)(2,1)}) %all-gather.10.cloned.1.call-update) | async-done | bytes 2097168 | tf_op jit(solution)/shard_map/all_gather | solution.py:16
  131.5 2.5 fusion.15
  134.0 44.6 %all-gather.12.cloned.1.call-done = bf16[1,4,2048,128]{3,2,1,0:T(8,128)(2,1)} async-done(((bf16[1,4,512,128]{3,2,1,0:T(8,128)(2,1)}), bf16[1,4,2048,128]{3,2,1,0:T(8,128)(2,1)}) %all-gather.12.cloned.1.call-update) | async-done | bytes 2097168 | tf_op jit(solution)/shard_map/all_gather | solution.py:24
  178.6 2.4 fusion.2
  181.0 0.0 copy-start
  181.0 25.8 %all-gather.14.cloned.1.call-done = bf16[1,2048,256]{2,1,0:T(8,128)(2,1)} async-done(((bf16[1,512,256]{2,1,0:T(8,128)(2,1)}), bf16[1,2048,256]{2,1,0:T(8,128)(2,1)}) %all-gather.14.cloned.1.call-update) | async-done | bytes 1048592 | tf_op jit(solution)/shard_map/all_gather | solution.py:26
  206.8 2.5 convolution_bitcast_fusion.1
  209.3 0.0 all-reduce.2.cloned.1.call-update
  209.4 0.0 reduce-scatter.3.cloned.1.call-start
  209.4 0.0 copy-start.1
  209.4 0.0 copy-done
  209.4 0.7 reduce-scatter.3.cloned.1.call-update
  210.1 0.2 reduce-scatter.5.cloned.1.call-start
  210.3 2.6 fusion.11
  213.0 0.0 copy-done.1
  213.0 2.2 convolution_bitcast_fusion
  215.2 0.0 reduce-scatter.5.cloned.1.call-update
  215.2 11.7 %all-reduce.2.cloned.1.call-done = f32[256,128]{0,1:T(8,128)} async-done(((f32[256,128]{0,1:T(8,128)}), f32[256,128]{0,1:T(8,128)}) %all-reduce.2.cloned.1.call-update) | async-done | bytes 131088 | tf_op jit(solution)/shard_map/psum | solution.py:47
  226.9 1.9 select_reduce_fusion.1
  228.7 0.1 copy.10
  229.5 11.7 %cholesky.17 = f32[128,128]{1,0:T(8,128)S(1)} custom-call(f32[128,128]{1,0:T(8,128)S(1)} %fusion.37), custom_call_target="Cholesky" | custom-call | tf_op jit(solution)/shard_map/jit(cholesky)/cholesky | solution.py:55
  241.3 0.6 compare_reduce_fusion
  241.9 0.7 fusion.32
  242.6 9.8 %custom-call.10 = f32[1,128,128]{1,2,0:T(8,128)S(1)} custom-call(f32[1,128,128]{2,1,0:T(8,128)S(1)} %fusion.32), custom_call_target="InvertDiagBlocksLowerTriangular" | custom-call | tf_op jit(solution)/shard_map/jit(_cho_solve)/triangular_solve | solution.py:57
  252.4 0.0 reduce-scatter.3.cloned.1.call-done
  252.4 2.0 copy.11
  254.5 0.0 reduce-scatter.5.cloned.1.call-done
  254.5 2.0 fusion.38
  256.5 0.6 fusion.34
  257.1 1.8 fusion.10
  (3 shorter events, 0.1 us)
Async XLA Ops:
  7.2 4.8 %copy-start.2 = (bf16[1,512,128]{2,1,0:T(8,128)(2,1)S(1)}, bf16[1,512,128]{2,1,0:T(8,128)(2,1)}, u32[]{:S(2)}) copy-start(bf16[1,512,128]{2,1,0:T(8,128)(2,1)} %param.11) | copy-start | bytes 393220
  7.2 16.4 %copy-start.3 = (s32[1,1,4]{2,1,0:T(1,128)S(1)}, s32[1,1,4]{2,1,0:T(1,128)}, u32[]{:S(2)}) copy-start(s32[1,1,4]{2,1,0:T(1,128)} %param.13) | copy-start | bytes 52
  7.2 51.4 %all-gather.6.cloned.1.call-start = ((), (), s32[]{:S(2)}) async-start(), calls=%async_computation.2 | async-start | bytes 2621440 | tf_op jit(solution)/shard_map/all_gather | solution.py:25
  9.3 85.1 %all-gather.8.cloned.1.call-start = ((), (), s32[]{:S(2)}) async-start(), calls=%async_computation.3 | async-start | bytes 2621440 | tf_op jit(solution)/shard_map/all_gather | solution.py:17
  10.1 121.4 %all-gather.10.cloned.1.call-start = ((), (), s32[]{:S(2)}) async-start(), calls=%async_computation.4 | async-start | bytes 2621440 | tf_op jit(solution)/shard_map/all_gather | solution.py:16
  10.8 167.8 %all-gather.12.cloned.1.call-start = ((), (), s32[]{:S(2)}) async-start(), calls=%async_computation.5 | async-start | bytes 2621440 | tf_op jit(solution)/shard_map/all_gather | solution.py:24
  11.4 195.4 %all-gather.14.cloned.1.call-start = ((), (), s32[]{:S(2)}) async-start(), calls=%async_computation.7 | async-start | bytes 1310720 | tf_op jit(solution)/shard_map/all_gather | solution.py:26
  12.0 214.9 %all-reduce.2.cloned.1.call-start = ((), (), s32[]{:S(2)}) async-start(), calls=%async_computation.8 | async-start | bytes 262144 | tf_op jit(solution)/shard_map/psum | solution.py:47
  181.0 28.4 %copy-start = (f32[128,2048,1]{1,0,2:T(8,128)}, f32[128,2048,1]{1,0,2:T(8,128)S(1)}, u32[]{:S(2)}) copy-start(f32[128,2048,1]{1,0,2:T(8,128)S(1)} %fusion.2) | copy-start | bytes 3145732
  209.4 43.1 %reduce-scatter.3.cloned.1.call-start = ((), (), s32[]{:S(2)}) async-start(), calls=%async_computation.6 | async-start | bytes 1572864 | tf_op jit(solution)/shard_map/reduce_scatter | solution.py:49
  209.4 3.5 %copy-start.1 = (bf16[1,4,2048,128]{3,2,1,0:T(8,128)(2,1)S(1)}, bf16[1,4,2048,128]{3,2,1,0:T(8,128)(2,1)}, u32[]{:S(2)}) copy-start(bf16[1,4,2048,128]{3,2,1,0:T(8,128)(2,1)} %all-gather.10.cloned.1.call-done) | copy-start | bytes 6291460
  210.1 44.3 %reduce-scatter.5.cloned.1.call-start = ((), (), s32[]{:S(2)}) async-start(), calls=%async_computation.9 | async-start | bytes 3145728 | tf_op jit(solution)/shard_map/reduce_scatter | solution.py:50
Sparse Core Ops, SparseCore 0:
  10.1 48.3 all-gather.5
  60.4 33.9 all-gather.7
  96.3 35.1 all-gather.9
  132.9 45.6 all-gather.11
  180.0 26.7 all-gather.13
  209.6 17.2 all-reduce.1
  229.1 9.6 reduce-scatter.2
  241.0 10.8 reduce-scatter.4
where the time goes:
time: 266 us
  waiting for transfers between devices  190 us (71%)
  other arithmetic  22.9 us (9%)
  matrix products  21.5 us (8%)
  between operations  14.9 us (6%)
  blocking collectives  11.5 us (4%)
  local copies, waits for them, and re-layouts  4.19 us (2%)
    all_gather x1, waiting for transfers between devices, body(): lax.all_gather(left_outer, 'col', axis=2, tiled=True)  44.6 us
    all_gather x1, waiting for transfers between devices, body(): lax.all_gather(right_inner, 'row', axis=2, tiled=True)  35.9 us
    all_gather x1, waiting for transfers between devices, body(): lax.all_gather(left_inner, 'col', axis=2, tiled=True)  35 us
    all_gather x1, waiting for transfers between devices, body(): lax.all_gather(right_outer, 'row', axis=2, tiled=True)  34.1 us
    all_gather x1, waiting for transfers between devices, body(): lax.all_gather(corange_test, 'col', axis=1, tiled=True)  25.8 us
    another operation x3, other arithmetic, body(): lower = jnp.linalg.cholesky(gram)  12.4 us
    psum x1, waiting for transfers between devices, body(): core = lax.psum(core_part, 'depth')  11.7 us
    all_gather x1, blocking collectives, body(): lax.all_gather(range_test, 'row', axis=1, tiled=True)  11.5 us
  transfers between devices with their start and end apart: 8, of which 6 were waited for; matrix products, arithmetic and copies ran while one was open for 15% of the time, Pallas kernels for 0%

commit v1 on v0

v1 whole, which is shorter than its diff:
```python
import functools

import jax
import jax.numpy as jnp
from jax import lax
from jax.experimental import pallas as pl
from jax.experimental.pallas import tpu as pltpu
from jax.sharding import PartitionSpec as P

F32 = jnp.float32
BF16 = jnp.bfloat16
HIGHEST = lax.Precision.HIGHEST
MESH = pl.DeviceIdType.MESH


def mm(a, b, contract=(1, 0), precision=None):
    dims = (((contract[0],), (contract[1],)), ((), ()))
    return lax.dot_general(a, b, dims, precision=precision, preferred_element_type=F32)


def guarded(cond, action):
    if cond is None:
        action()
    else:
        pl.when(cond)(action)


def inverse_schedule(rank):
    low = 1.0 / (rank / 0.05 + 1.0)
    low *= 0.999
    start = 2.0 / (1.0 + low)
    err = 1.0 - low * start
    scales = []
    while err > 1e-8:
        scales.append(2.0 / (2.0 - err * err))
        err = err * err / (2.0 - err * err)
    return start, scales


def kernel(
    sizes,
    lo, li, ro, ri, rt, ct, mask,
    out_range, out_corange,
    lig, rig, pp, ppr, probe, tp, tpr, test, crt, cps, cpr, zz,
    rps, rpr, rsend, rout, qps, qpr, qsend, qout,
    li_l, li_r, li_in, ri_s, ri_in,
    pp_s, pp_in, pr_s, pr_in, tp_s, tp_in, te_s, te_in,
    cr_s, cr_in, cp_s, cp_in, z_s, z_in,
    rp_s, rp_in, ro_s, ro_in, qp_s, qp_in, qo_s, qo_in,
):
    R, C, D, K = sizes
    KR, KC = K // R, K // C
    rank = lo.shape[2]
    r, c, d = lax.axis_index("row"), lax.axis_index("col"), lax.axis_index("depth")
    pending = []

    def copy(src, dst, send, recv, dev, cond=None):
        op = pltpu.make_async_remote_copy(
            src_ref=src, dst_ref=dst, send_sem=send, recv_sem=recv,
            device_id=dev, device_id_type=MESH,
        )
        guarded(cond, op.start)
        pending.append((cond, op))

    def arrive(dst, send, recv, cond=None):
        op = pltpu.make_async_remote_copy(
            src_ref=dst, dst_ref=dst, send_sem=send, recv_sem=recv,
            device_id=(r, c, d), device_id_type=MESH,
        )
        guarded(cond, op.wait_recv)

    def row_peer(o):
        return lax.rem(r + o, R)

    def col_peer(o):
        return lax.rem(c + o, C)

    def depth_peer(o):
        return lax.rem(d + o, D)

    bar = pltpu.get_barrier_semaphore()

    @pl.loop(1, R * D)
    def _(o):
        n = lax.rem(r * D + d + o, R * D)
        pl.semaphore_signal(bar, inc=1, device_id=(n // D, c, lax.rem(n, D)), device_id_type=MESH)

    @pl.loop(1, C * D)
    def _(o):
        n = lax.rem(c * D + d + o, C * D)
        pl.semaphore_signal(bar, inc=1, device_id=(r, n // D, lax.rem(n, D)), device_id_type=MESH)

    pl.semaphore_wait(bar, R * D + C * D - 2)

    def send_li(k):
        copy(li.at[k], lig.at[c, k], li_l.at[0, k], li_in.at[c, k], (r, c - 1, d), c > 0)
        copy(li.at[k], lig.at[c, k], li_r.at[0, k], li_in.at[c, k], (r, c + 1, d), c < C - 1)

    def send_ri(k):
        for o in range(1, R):
            copy(ri.at[k], rig.at[r, k], ri_s.at[o, k], ri_in.at[r, k], (row_peer(o), c, d))

    def forward_li(o, k):
        far = c + o
        cond = far < C
        arrive(lig.at[far, k], li_l.at[o, k], li_in.at[far, k], cond)
        if o < C - 1:
            copy(lig.at[far, k], lig.at[far, k], li_l.at[o, k], li_in.at[far, k],
                 (r, c - 1, d), jnp.logical_and(cond, c > 0))
        near = c - o
        cond = near >= 0
        arrive(lig.at[near, k], li_r.at[o, k], li_in.at[near, k], cond)
        if o < C - 1:
            copy(lig.at[near, k], lig.at[near, k], li_r.at[o, k], li_in.at[near, k],
                 (r, c + 1, d), jnp.logical_and(cond, c < C - 1))

    half = (K + 1) // 2
    for k in range(half):
        send_li(k)
        send_ri(k)

    for k in range(K):
        tp[k] = mm(lo[k], ct[...], (0, 0))
    for o in range(1, C):
        n = col_peer(o)
        copy(tp.at[pl.ds(n * KC, KC)], tpr.at[c], tp_s.at[o], tp_in.at[c], (r, n, d))
    for k in range(K):
        pp[k] = mm(rt[...], ro[k], (0, 0))
    for o in range(1, R):
        n = row_peer(o)
        copy(pp.at[pl.ds(n * KR, KR)], ppr.at[r], pp_s.at[o], pp_in.at[r], (n, c, d))
    for k in range(half, K):
        send_li(k)
        send_ri(k)
    lig[c] = li[...]
    rig[r] = ri[...]

    for k in range(K):
        forward_li(1, k)

    total = tp[pl.ds(c * KC, KC)]
    for o in range(1, C):
        n = col_peer(o)
        arrive(tpr.at[n], tp_s.at[o], tp_in.at[n])
        total = total + tpr[n]
    test[c] = total.astype(BF16)
    for o in range(1, C):
        copy(test.at[c], test.at[c], te_s.at[o], te_in.at[c], (r, col_peer(o), d))
    total = pp[pl.ds(r * KR, KR)]
    for o in range(1, R):
        n = row_peer(o)
        arrive(ppr.at[n], pp_s.at[o], pp_in.at[n])
        total = total + ppr[n]
    probe[r] = total.astype(BF16)
    for o in range(1, R):
        copy(probe.at[r], probe.at[r], pr_s.at[o], pr_in.at[r], (row_peer(o), c, d))

    for o in range(2, C - 1):
        for k in range(K):
            forward_li(o, k)

    for k in range(K):
        for o in range(1, R):
            n = row_peer(o)
            arrive(rig.at[n, k], ri_s.at[o, k], ri_in.at[n, k])
    for o in range(1, R):
        n = row_peer(o)
        arrive(probe.at[n], pr_s.at[o], pr_in.at[n])
    for o in range(1, C):
        n = col_peer(o)
        arrive(test.at[n], te_s.at[o], te_in.at[n])

    scale = (K * D) ** -0.5
    core_left = []
    core_part = None
    for k in range(K):
        if C > 2:
            forward_li(C - 1, k)
        cross = None
        for b in range(C):
            term = mm(rig[b, k], lig[b, k], (0, 0))
            cross = term if cross is None else cross + term
        cross = cross.astype(BF16)
        weight = mask[0, 0, k].astype(F32) * scale
        right = (mm(probe[k // KR, k % KR], cross) * weight).astype(BF16)
        crt[c, k] = right
        for o in range(1, C):
            copy(crt.at[c, k], crt.at[c, k], cr_s.at[o, k], cr_in.at[c, k], (r, col_peer(o), d))
        test_k = test[k // KC, k % KC]
        core_left.append((mm(cross, test_k) * weight).astype(BF16))
        term = mm(right, test_k)
        core_part = term if core_part is None else core_part + term

    cps[...] = core_part
    for o in range(1, D):
        copy(cps, cpr.at[d], cp_s.at[o], cp_in.at[d], (r, c, depth_peer(o)))
    cpr[d] = core_part
    for o in range(1, D):
        n = depth_peer(o)
        arrive(cpr.at[n], cp_s.at[o], cp_in.at[n])
    core = cpr[0]
    for n in range(1, D):
        core = core + cpr[n]

    gram = mm(core, core, (1, 1), HIGHEST)
    eye = (
        lax.broadcasted_iota(jnp.int32, (rank, rank), 0)
        == lax.broadcasted_iota(jnp.int32, (rank, rank), 1)
    ).astype(F32)
    trace = jnp.sum(gram * eye)
    ridge = 0.05 * trace / rank + 1e-05
    gram = gram + ridge * eye
    start, scales = inverse_schedule(rank)
    first = start / jnp.broadcast_to(trace + ridge, (rank, rank))
    inv = (scales[0] * first) * (2.0 * eye - first * gram)
    for factor in scales[1:]:
        step = 2.0 * eye - mm(gram, inv, precision=HIGHEST)
        inv = factor * mm(inv, step, precision=HIGHEST)
    weights = (mm(inv, core, precision=HIGHEST) * rank**0.5).astype(BF16)

    for k in range(K):
        zz[r, k] = mm(core_left[k], weights, (1, 1)).astype(BF16)
    for o in range(1, R):
        copy(zz.at[r], zz.at[r], z_s.at[o], z_in.at[r], (row_peer(o), c, d))

    part_l = lo.shape[1] // D
    for o in range(C):
        j = col_peer(o)
        if o > 0:
            for k in range(K):
                arrive(crt.at[j, k], cr_s.at[o, k], cr_in.at[j, k])
        total = None
        for k in range(K):
            term = mm(lo[k], crt[j, k], (1, 1))
            total = term if total is None else total + term
        for n in range(D):
            rps[n, j] = total[n * part_l:(n + 1) * part_l]
    for o in range(1, D):
        n = depth_peer(o)
        copy(rps.at[n], rpr.at[d], rp_s.at[o], rp_in.at[d], (r, c, n))
    total = rps[d]
    for o in range(1, D):
        n = depth_peer(o)
        arrive(rpr.at[n], rp_s.at[o], rp_in.at[n])
        total = total + rpr[n]
    rsend[...] = total.astype(BF16)
    place = c * D + d
    owner, slot = place // C, lax.rem(place, C)
    for o in range(1, C):
        j = col_peer(o)
        copy(rsend.at[j], rout.at[slot], ro_s.at[o], ro_in.at[slot], (r, j, owner))
    copy(rsend.at[c], rout.at[slot], ro_s.at[0], ro_in.at[slot], (r, c, owner), owner != d)

    part_r = ro.shape[1] // D
    for o in range(R):
        i = row_peer(o)
        if o > 0:
            arrive(zz.at[i], z_s.at[o], z_in.at[i])
        total = None
        for k in range(K):
            term = mm(ro[k], zz[i, k])
            total = term if total is None else total + term
        for n in range(D):
            qps[n, i] = total[n * part_r:(n + 1) * part_r]
    for o in range(1, D):
        n = depth_peer(o)
        copy(qps.at[n], qpr.at[d], qp_s.at[o], qp_in.at[d], (r, c, n))
    total = qps[d]
    for o in range(1, D):
        n = depth_peer(o)
        arrive(qpr.at[n], qp_s.at[o], qp_in.at[n])
        total = total + qpr[n]
    qsend[...] = total.astype(BF16)
    place_q = r * D + d
    owner_q, slot_q = place_q // R, lax.rem(place_q, R)
    for o in range(1, R):
        i = row_peer(o)
        copy(qsend.at[i], qout.at[slot_q], qo_s.at[o], qo_in.at[slot_q], (i, c, owner_q))
    copy(qsend.at[r], qout.at[slot_q], qo_s.at[0], qo_in.at[slot_q], (r, c, owner_q), owner_q != d)

    @pl.when(owner == d)
    def _():
        rout[slot] = rsend[c]

    @pl.when(owner_q == d)
    def _():
        qout[slot_q] = qsend[r]

    for q in range(C):
        src = d * C + q
        mine = jnp.logical_and(src // D == c, lax.rem(src, D) == d)
        arrive(rout.at[q], ro_s.at[0], ro_in.at[q], jnp.logical_not(mine))
        out_range[q * part_l:(q + 1) * part_l, :] = rout[q].astype(F32)
    for q in range(R):
        src = d * R + q
        mine = jnp.logical_and(src // D == r, lax.rem(src, D) == d)
        arrive(qout.at[q], qo_s.at[0], qo_in.at[q], jnp.logical_not(mine))
        out_corange[q * part_r:(q + 1) * part_r, :] = qout[q].astype(F32)
    for cond, op in pending:
        guarded(cond, op.wait_send)


def body(sizes, left_outer, left_inner, right_outer, right_inner, range_test, corange_test, product_mask):
    R, C, D = sizes
    K, BL, rank = left_outer.shape[1:]
    BR = right_outer.shape[2]
    sketch = corange_test.shape[2]
    assert R == C and K % R == 0 and BL % D == 0
    KR, KC = K // R, K // C
    dma = pltpu.SemaphoreType.DMA
    vmem = pltpu.VMEM
    scratch = [
        vmem((C, K, BL, rank), BF16),
        vmem((R, K, BR, rank), BF16),
        vmem((K, rank, rank), F32),
        vmem((R, KR, rank, rank), F32),
        vmem((R, KR, rank, rank), BF16),
        vmem((K, rank, sketch), F32),
        vmem((C, KC, rank, sketch), F32),
        vmem((C, KC, rank, sketch), BF16),
        vmem((C, K, rank, rank), BF16),
        vmem((rank, sketch), F32),
        vmem((D, rank, sketch), F32),
        vmem((R, K, rank, rank), BF16),
        vmem((D, C, BL // D, rank), F32),
        vmem((D, C, BL // D, rank), F32),
        vmem((C, BL // D, rank), BF16),
        vmem((C, BL // D, rank), BF16),
        vmem((D, R, BR // D, rank), F32),
        vmem((D, R, BR // D, rank), F32),
        vmem((R, BR // D, rank), BF16),
        vmem((R, BR // D, rank), BF16),
        dma((C, K)), dma((C, K)), dma((C, K)), dma((R, K)), dma((R, K)),
        dma((R,)), dma((R,)), dma((R,)), dma((R,)),
        dma((C,)), dma((C,)), dma((C,)), dma((C,)),
        dma((C, K)), dma((C, K)), dma((D,)), dma((D,)), dma((R,)), dma((R,)),
        dma((D,)), dma((D,)), dma((C,)), dma((C,)),
        dma((D,)), dma((D,)), dma((R,)), dma((R,)),
    ]
    tile = BL * C
    whole = pl.BlockSpec(memory_space=pltpu.VMEM)
    out = jax.ShapeDtypeStruct((tile // D, rank), F32)
    range_rows, corange_rows = pl.pallas_call(
        functools.partial(kernel, (R, C, D, K)),
        out_shape=(out, out),
        in_specs=[whole] * 6 + [pl.BlockSpec(memory_space=pltpu.SMEM)],
        out_specs=(whole, whole),
        scratch_shapes=scratch,
        compiler_params=pltpu.CompilerParams(
            collective_id=0, has_side_effects=True, vmem_limit_bytes=60 * 1024 * 1024
        ),
    )(left_outer[0], left_inner[0], right_outer[0], right_inner[0],
      range_test[0], corange_test[0], product_mask)
    return range_rows[None, None], corange_rows[None, None]


def solution(mesh):
    sizes = tuple(mesh.shape[name] for name in ("row", "col", "depth"))
    return jax.shard_map(
        functools.partial(body, sizes),
        mesh=mesh,
        in_specs=(
            P("row", "depth", "col", None),
            P("row", "depth", "col", None),
            P("col", "depth", "row", None),
            P("col", "depth", "row", None),
            P("col", "row", None),
            P("row", "col", None),
            P("row", "col", "depth"),
        ),
        out_specs=(P("row", "col", "depth", None), P("row", "col", "depth", None)),
        check_vma=False,
    )
```

time: 266 us -> 88.1 us (0.33)
  waiting for transfers between devices: 190 us -> 0 us
  Pallas kernels: 0 us -> 84.6 us
  other arithmetic: 22.9 us -> 0 us
  matrix products: 21.5 us -> 0 us
  between operations: 14.9 us -> 0.65 us
  blocking collectives: 11.5 us -> 0 us
    all_gather x5 -> x0, waiting for transfers between devices: 175 us -> none  [the longest x1 44.6 us: body(): lax.all_gather(left_outer, 'col', axis=2, tiled=True)]
    pallas_call x0 -> x1, Pallas kernels: none -> 84.6 us  [body(): pl.pallas_call(functools.partial(kernel, (R, C, D, K)), out_shape=(out, o...]
    another operation x5 -> x0, other arithmetic: 22.9 us -> none  [the longest x3 12.4 us: body(): lower = jnp.linalg.cholesky(gram)]
    dot_general x8 -> x0, matrix products: 19.1 us -> none  [the longest x1 2.92 us: body(): jnp.einsum('kbr,kbs->krs', inner_left[0], inner_right[0], preferred_eleme...]
    psum x1 -> x0, waiting for transfers between devices: 11.7 us -> none  [body(): core = lax.psum(core_part, 'depth')]
    all_gather x1 -> x0, blocking collectives: 11.5 us -> none  [body(): lax.all_gather(range_test, 'row', axis=1, tiled=True)]
    unnamed x8 -> x0, waiting for transfers between devices: 3.16 us -> none
  transfers between devices with their start and end apart: 8 -> 0, of which waited for: 6 -> 0; matrix products, arithmetic and copies ran while one was open for 15% -> 0% of each run, Pallas kernels for 0% -> 0%
where the time goes in v1:
time: 88.1 us; the launch traced here: 88 us
  Pallas kernels  84.6 us (96%)
  local copies, waits for them, and re-layouts  2.72 us (3%)
    pallas_call x1, Pallas kernels, body(): pl.pallas_call(functools.partial(kernel, (R, C, D, K)), out_shape=(out, o...  84.6 us
    unnamed x4, local copies, waits for them, and re-layouts  2.72 us

profile of v1, /device:TPU:0, one launch (start us, length us, event | category | flops | bytes accessed | tf_op | source)
XLA Modules:
  0.0 88.0 jit_solution(8686846537580590605)
XLA Ops:
  0.6 84.6 %shard_map.86 = (f32[1024,128]{1,0:T(8,128)}, f32[1024,128]{1,0:T(8,128)}) custom-call(bf16[4,512,128]{2,1,0:T(8,128)(2,1)} %bitcast.10, bf16[4,512,128]{2,1,0:T(8,128)(2,1)} %bitcast.11, bf16[4,512,128]{2,1,0:T(8,128)(2,1)} %bitcast.12, bf16[4,512,128]{2,1,0:T(8,128)(2,1)} %bitcast.13, bf16[512,128]{1,0:T(8,128)(2,1)} %bitcast.15, ...), custom_call_target="tpu_custom_call" | custom-call | tf_op jit(solution)/shard_map/pallas_call | solution.py:343
  85.2 0.0 copy-start
  85.2 1.9 %copy.11 = f32[1,1,1024,128]{3,2,1,0:T(8,128)} copy(f32[1,1,1024,128]{3,2,1,0:T(8,128)} %bitcast.9) | data formatting | bytes 1048576
  87.2 0.0 copy-done
  87.2 0.8 copy.12
Async XLA Ops:
  85.2 1.9 %copy-start = (f32[1024,128]{1,0:T(8,128)S(1)}, f32[1024,128]{1,0:T(8,128)}, u32[]{:S(2)}) copy-start(f32[1024,128]{1,0:T(8,128)} %get-tuple-element.5) | copy-start | bytes 1572868

commit v2 on v1

--- a/solution.py
+++ b/solution.py
@@ -98,7 +98,7 @@
 
     def send_ri(k):
         for o in range(1, R):
-            copy(ri.at[k], rig.at[r, k], ri_s.at[o, k], ri_in.at[r, k], (row_peer(o), c, d))
+            copy(rig.at[r, k], rig.at[r, k], ri_s.at[o, k], ri_in.at[r, k], (row_peer(o), c, d))
 
     def forward_li(o, k):
         far = c + o
@@ -117,23 +117,28 @@
     half = (K + 1) // 2
     for k in range(half):
         send_li(k)
+    for k in range(half):
+        rig[r, k] = ri[k].T
         send_ri(k)
 
-    for k in range(K):
-        tp[k] = mm(lo[k], ct[...], (0, 0))
+    ct_rows = ct[...].T
+    for k in range(K):
+        tp[k] = mm(ct_rows, lo[k])
     for o in range(1, C):
         n = col_peer(o)
         copy(tp.at[pl.ds(n * KC, KC)], tpr.at[c], tp_s.at[o], tp_in.at[c], (r, n, d))
-    for k in range(K):
-        pp[k] = mm(rt[...], ro[k], (0, 0))
+    rt_rows = rt[...].T
+    for k in range(K):
+        pp[k] = mm(rt_rows, ro[k])
     for o in range(1, R):
         n = row_peer(o)
         copy(pp.at[pl.ds(n * KR, KR)], ppr.at[r], pp_s.at[o], pp_in.at[r], (n, c, d))
     for k in range(half, K):
         send_li(k)
+    for k in range(half, K):
+        rig[r, k] = ri[k].T
         send_ri(k)
     lig[c] = li[...]
-    rig[r] = ri[...]
 
     for k in range(K):
         forward_li(1, k)
@@ -178,17 +183,19 @@
             forward_li(C - 1, k)
         cross = None
         for b in range(C):
-            term = mm(rig[b, k], lig[b, k], (0, 0))
+            term = mm(rig[b, k], lig[b, k])
             cross = term if cross is None else cross + term
         cross = cross.astype(BF16)
         weight = mask[0, 0, k].astype(F32) * scale
         right = (mm(probe[k // KR, k % KR], cross) * weight).astype(BF16)
-        crt[c, k] = right
+        lanes = pl.ds(k * rank, rank)
+        crt[c, :, lanes] = right
         for o in range(1, C):
-            copy(crt.at[c, k], crt.at[c, k], cr_s.at[o, k], cr_in.at[c, k], (r, col_peer(o), d))
+            copy(crt.at[c, :, lanes], crt.at[c, :, lanes], cr_s.at[o, k], cr_in.at[c, k],
+                 (r, col_peer(o), d))
         test_k = test[k // KC, k % KC]
-        core_left.append((mm(cross, test_k) * weight).astype(BF16))
-        term = mm(right, test_k)
+        core_left.append((mm(cross, test_k, (1, 1)) * weight).astype(BF16))
+        term = mm(right, test_k, (1, 1))
         core_part = term if core_part is None else core_part + term
 
     cps[...] = core_part
@@ -219,64 +226,64 @@
     weights = (mm(inv, core, precision=HIGHEST) * rank**0.5).astype(BF16)
 
     for k in range(K):
-        zz[r, k] = mm(core_left[k], weights, (1, 1)).astype(BF16)
-    for o in range(1, R):
-        copy(zz.at[r], zz.at[r], z_s.at[o], z_in.at[r], (row_peer(o), c, d))
+        rows = pl.ds(k * rank, rank)
+        zz[r, rows] = mm(core_left[k], weights, (1, 1)).astype(BF16)
+        for o in range(1, R):
+            copy(zz.at[r, rows], zz.at[r, rows], z_s.at[o, k], z_in.at[r, k], (row_peer(o), c, d))
 
     part_l = lo.shape[1] // D
+    place = c * D + d
+    owner, slot = place // C, lax.rem(place, C)
+    lo_all = jnp.concatenate([lo[k] for k in range(K)], axis=1)
     for o in range(C):
         j = col_peer(o)
         if o > 0:
             for k in range(K):
-                arrive(crt.at[j, k], cr_s.at[o, k], cr_in.at[j, k])
-        total = None
-        for k in range(K):
-            term = mm(lo[k], crt[j, k], (1, 1))
-            total = term if total is None else total + term
+                lanes = pl.ds(k * rank, rank)
+                arrive(crt.at[j, :, lanes], cr_s.at[o, k], cr_in.at[j, k])
+        total = mm(lo_all, crt[j], (1, 1))
         for n in range(D):
             rps[n, j] = total[n * part_l:(n + 1) * part_l]
-    for o in range(1, D):
-        n = depth_peer(o)
-        copy(rps.at[n], rpr.at[d], rp_s.at[o], rp_in.at[d], (r, c, n))
-    total = rps[d]
-    for o in range(1, D):
-        n = depth_peer(o)
-        arrive(rpr.at[n], rp_s.at[o], rp_in.at[n])
-        total = total + rpr[n]
-    rsend[...] = total.astype(BF16)
-    place = c * D + d
-    owner, slot = place // C, lax.rem(place, C)
-    for o in range(1, C):
+        for e in range(1, D):
+            n = depth_peer(e)
+            copy(rps.at[n, j], rpr.at[d, j], rp_s.at[e, o], rp_in.at[d, j], (r, c, n))
+    for o in range(C):
         j = col_peer(o)
-        copy(rsend.at[j], rout.at[slot], ro_s.at[o], ro_in.at[slot], (r, j, owner))
-    copy(rsend.at[c], rout.at[slot], ro_s.at[0], ro_in.at[slot], (r, c, owner), owner != d)
+        total = rps[d, j]
+        for e in range(1, D):
+            n = depth_peer(e)
+            arrive(rpr.at[n, j], rp_s.at[e, o], rp_in.at[n, j])
+            total = total + rpr[n, j]
+        rsend[j] = total.astype(BF16)
+        copy(rsend.at[j], rout.at[slot], ro_s.at[o], ro_in.at[slot], (r, j, owner),
+             owner != d if o == 0 else None)
 
     part_r = ro.shape[1] // D
+    place_q = r * D + d
+    owner_q, slot_q = place_q // R, lax.rem(place_q, R)
+    ro_all = jnp.concatenate([ro[k] for k in range(K)], axis=1)
     for o in range(R):
         i = row_peer(o)
         if o > 0:
-            arrive(zz.at[i], z_s.at[o], z_in.at[i])
-        total = None
-        for k in range(K):
-            term = mm(ro[k], zz[i, k])
-            total = term if total is None else total + term
+            for k in range(K):
+                rows = pl.ds(k * rank, rank)
+                arrive(zz.at[i, rows], z_s.at[o, k], z_in.at[i, k])
+        total = mm(ro_all, zz[i])
         for n in range(D):
             qps[n, i] = total[n * part_r:(n + 1) * part_r]
-    for o in range(1, D):
-        n = depth_peer(o)
-        copy(qps.at[n], qpr.at[d], qp_s.at[o], qp_in.at[d], (r, c, n))
-    total = qps[d]
-    for o in range(1, D):
-        n = depth_peer(o)
-        arrive(qpr.at[n], qp_s.at[o], qp_in.at[n])
-        total = total + qpr[n]
-    qsend[...] = total.astype(BF16)
-    place_q = r * D + d
-    owner_q, slot_q = place_q // R, lax.rem(place_q, R)
-    for o in range(1, R):
+        for e in range(1, D):
+            n = depth_peer(e)
+            copy(qps.at[n, i], qpr.at[d, i], qp_s.at[e, o], qp_in.at[d, i], (r, c, n))
+    for o in range(R):
         i = row_peer(o)
-        copy(qsend.at[i], qout.at[slot_q], qo_s.at[o], qo_in.at[slot_q], (i, c, owner_q))
-    copy(qsend.at[r], qout.at[slot_q], qo_s.at[0], qo_in.at[slot_q], (r, c, owner_q), owner_q != d)
+        total = qps[d, i]
+        for e in range(1, D):
+            n = depth_peer(e)
+            arrive(qpr.at[n, i], qp_s.at[e, o], qp_in.at[n, i])
+            total = total + qpr[n, i]
+        qsend[i] = total.astype(BF16)
+        copy(qsend.at[i], qout.at[slot_q], qo_s.at[o], qo_in.at[slot_q], (i, c, owner_q),
+             owner_q != d if o == 0 else None)
 
     @pl.when(owner == d)
     def _():
@@ -290,12 +297,12 @@
         src = d * C + q
         mine = jnp.logical_and(src // D == c, lax.rem(src, D) == d)
         arrive(rout.at[q], ro_s.at[0], ro_in.at[q], jnp.logical_not(mine))
-        out_range[q * part_l:(q + 1) * part_l, :] = rout[q].astype(F32)
+        out_range[q * part_l:(q + 1) * part_l, :] = rout[q]
     for q in range(R):
         src = d * R + q
         mine = jnp.logical_and(src // D == r, lax.rem(src, D) == d)
         arrive(qout.at[q], qo_s.at[0], qo_in.at[q], jnp.logical_not(mine))
-        out_corange[q * part_r:(q + 1) * part_r, :] = qout[q].astype(F32)
+        out_corange[q * part_r:(q + 1) * part_r, :] = qout[q]
     for cond, op in pending:
         guarded(cond, op.wait_send)
 
@@ -311,17 +318,17 @@
     vmem = pltpu.VMEM
     scratch = [
         vmem((C, K, BL, rank), BF16),
-        vmem((R, K, BR, rank), BF16),
+        vmem((R, K, rank, BR), BF16),
         vmem((K, rank, rank), F32),
         vmem((R, KR, rank, rank), F32),
         vmem((R, KR, rank, rank), BF16),
-        vmem((K, rank, sketch), F32),
-        vmem((C, KC, rank, sketch), F32),
-        vmem((C, KC, rank, sketch), BF16),
-        vmem((C, K, rank, rank), BF16),
+        vmem((K, sketch, rank), F32),
+        vmem((C, KC, sketch, rank), F32),
+        vmem((C, KC, sketch, rank), BF16),
+        vmem((C, rank, K * rank), BF16),
         vmem((rank, sketch), F32),
         vmem((D, rank, sketch), F32),
-        vmem((R, K, rank, rank), BF16),
+        vmem((R, K * rank, rank), BF16),
         vmem((D, C, BL // D, rank), F32),
         vmem((D, C, BL // D, rank), F32),
         vmem((C, BL // D, rank), BF16),
@@ -333,13 +340,13 @@
         dma((C, K)), dma((C, K)), dma((C, K)), dma((R, K)), dma((R, K)),
         dma((R,)), dma((R,)), dma((R,)), dma((R,)),
         dma((C,)), dma((C,)), dma((C,)), dma((C,)),
-        dma((C, K)), dma((C, K)), dma((D,)), dma((D,)), dma((R,)), dma((R,)),
-        dma((D,)), dma((D,)), dma((C,)), dma((C,)),
-        dma((D,)), dma((D,)), dma((R,)), dma((R,)),
+        dma((C, K)), dma((C, K)), dma((D,)), dma((D,)), dma((R, K)), dma((R, K)),
+        dma((D, C)), dma((D, C)), dma((C,)), dma((C,)),
+        dma((D, R)), dma((D, R)), dma((R,)), dma((R,)),
     ]
     tile = BL * C
     whole = pl.BlockSpec(memory_space=pltpu.VMEM)
-    out = jax.ShapeDtypeStruct((tile // D, rank), F32)
+    out = jax.ShapeDtypeStruct((tile // D, rank), BF16)
     range_rows, corange_rows = pl.pallas_call(
         functools.partial(kernel, (R, C, D, K)),
         out_shape=(out, out),
@@ -351,7 +358,7 @@
         ),
     )(left_outer[0], left_inner[0], right_outer[0], right_inner[0],
       range_test[0], corange_test[0], product_mask)
-    return range_rows[None, None], corange_rows[None, None]
+    return range_rows[None, None].astype(F32), corange_rows[None, None].astype(F32)
 
 
 def solution(mesh):

time: 88.1 us -> 86.2 us (0.978)
  local copies, waits for them, and re-layouts: 2.72 us -> 0 us
  other arithmetic: 0 us -> 2.07 us
  Pallas kernels: 84.6 us -> 83.4 us
    unnamed x4 -> x0, local copies, waits for them, and re-layouts: 2.72 us -> none
    convert_element_type x0 -> x1, other arithmetic: none -> 2.07 us  [body(): corange_rows[None, None].astype(F32)]
    pallas_call x1, Pallas kernels: 84.6 us -> 83.4 us  [body(): pl.pallas_call(functools.partial(kernel, (R, C, D, K)), out_shape=(out, o...]
where the time goes in v2:
time: 86.2 us; the launch traced here: 86.1 us
  Pallas kernels  83.4 us (97%)
  other arithmetic  2.07 us (2%)
    pallas_call x1, Pallas kernels, body(): pl.pallas_call(functools.partial(kernel, (R, C, D, K)), out_shape=(out, o...  83.4 us
    convert_element_type x1, other arithmetic, body(): corange_rows[None, None].astype(F32)  2.07 us

profile of v2, /device:TPU:0, one launch (start us, length us, event | category | flops | bytes accessed | tf_op | source)
XLA Modules:
  0.0 86.1 jit_solution(2841778688397679672)
XLA Ops:
  0.6 83.4 %shard_map.86 = (bf16[1024,128]{1,0:T(8,128)(2,1)}, bf16[1024,128]{1,0:T(8,128)(2,1)}) custom-call(bf16[4,512,128]{2,1,0:T(8,128)(2,1)} %bitcast.12, bf16[4,512,128]{2,1,0:T(8,128)(2,1)} %bitcast.13, bf16[4,512,128]{2,1,0:T(8,128)(2,1)} %bitcast.14, bf16[4,512,128]{2,1,0:T(8,128)(2,1)} %bitcast.15, bf16[512,128]{1,0:T(8,128)(2,1)} %bitcast.17, ...), custom_call_target="tpu_custom_call" | custom-call | tf_op jit(solution)/shard_map/pallas_call | solution.py:350
  84.0 2.1 %bitcast_convert_fusion = (f32[1,1,1024,128]{3,2,1,0:T(8,128)}, f32[1,1,1024,128]{3,2,1,0:T(8,128)}) fusion(bf16[1024,128]{1,0:T(8,128)(2,1)} %get-tuple-element.5, bf16[1024,128]{1,0:T(8,128)(2,1)} %get-tuple-element.4), kind=kLoop, calls=%fused_computation | loop fusion | flops 262144 | bytes 1572864 | tf_op jit(solution)/shard_map/convert_element_type | solution.py:361

commit v3 on v2

--- a/solution.py
+++ b/solution.py
@@ -42,11 +42,11 @@
     lo, li, ro, ri, rt, ct, mask,
     out_range, out_corange,
     lig, rig, pp, ppr, probe, tp, tpr, test, crt, cps, cpr, zz,
-    rps, rpr, rsend, rout, qps, qpr, qsend, qout,
+    rps, rpr, rsend, rout, qps, qpr, qsend, qout, ext, xs, xr, cx,
     li_l, li_r, li_in, ri_s, ri_in,
     pp_s, pp_in, pr_s, pr_in, tp_s, tp_in, te_s, te_in,
     cr_s, cr_in, cp_s, cp_in, z_s, z_in,
-    rp_s, rp_in, ro_s, ro_in, qp_s, qp_in, qo_s, qo_in,
+    rp_s, rp_in, ro_s, ro_in, qp_s, qp_in, qo_s, qo_in, ext_s, ext_in, x_s,
 ):
     R, C, D, K = sizes
     KR, KC = K // R, K // C
@@ -92,27 +92,39 @@
 
     pl.semaphore_wait(bar, R * D + C * D - 2)
 
+    moved = K - 1 if C >= 4 else K
+    at_end = jnp.logical_or(c == 0, c == C - 1)
+    inside = jnp.logical_and(c > 0, c < C - 1)
+    helper = jnp.logical_or(c == 1, c == C - 2)
+    near_end = 1 + (c // (C - 1)) * (C - 3)
+    served = ((c - 1) // max(C - 3, 1)) * (C - 1)
+
     def send_li(k):
-        copy(li.at[k], lig.at[c, k], li_l.at[0, k], li_in.at[c, k], (r, c - 1, d), c > 0)
-        copy(li.at[k], lig.at[c, k], li_r.at[0, k], li_in.at[c, k], (r, c + 1, d), c < C - 1)
+        skip = 1 if k == moved else 0
+        copy(li.at[k], lig.at[c, k], li_l.at[0, k], li_in.at[c, k], (r, c - 1, d), c > skip)
+        copy(li.at[k], lig.at[c, k], li_r.at[0, k], li_in.at[c, k], (r, c + 1, d), c < C - 1 - skip)
 
     def send_ri(k):
+        if k == moved:
+            copy(rig.at[r, k], ext.at[r], ext_s.at[0], ext_in.at[r], (r, near_end, d), at_end)
         for o in range(1, R):
-            copy(rig.at[r, k], rig.at[r, k], ri_s.at[o, k], ri_in.at[r, k], (row_peer(o), c, d))
+            copy(rig.at[r, k], rig.at[r, k], ri_s.at[o, k], ri_in.at[r, k], (row_peer(o), c, d),
+                 inside if k == moved else None)
 
     def forward_li(o, k):
+        skip = 1 if k == moved else 0
         far = c + o
-        cond = far < C
+        cond = jnp.logical_and(far < C, c >= skip)
         arrive(lig.at[far, k], li_l.at[o, k], li_in.at[far, k], cond)
         if o < C - 1:
             copy(lig.at[far, k], lig.at[far, k], li_l.at[o, k], li_in.at[far, k],
-                 (r, c - 1, d), jnp.logical_and(cond, c > 0))
+                 (r, c - 1, d), jnp.logical_and(cond, c > skip))
         near = c - o
-        cond = near >= 0
+        cond = jnp.logical_and(near >= 0, c < C - skip)
         arrive(lig.at[near, k], li_r.at[o, k], li_in.at[near, k], cond)
         if o < C - 1:
             copy(lig.at[near, k], lig.at[near, k], li_r.at[o, k], li_in.at[near, k],
-                 (r, c + 1, d), jnp.logical_and(cond, c < C - 1))
+                 (r, c + 1, d), jnp.logical_and(cond, c < C - 1 - skip))
 
     half = (K + 1) // 2
     for k in range(half):
@@ -142,6 +154,11 @@
 
     for k in range(K):
         forward_li(1, k)
+
+    if moved < K:
+        arrive(ext.at[r], ext_s.at[0], ext_in.at[r], helper)
+        for o in range(1, R):
+            copy(ext.at[r], ext.at[r], ext_s.at[o], ext_in.at[r], (row_peer(o), c, d), helper)
 
     total = tp[pl.ds(c * KC, KC)]
     for o in range(1, C):
@@ -167,7 +184,30 @@
     for k in range(K):
         for o in range(1, R):
             n = row_peer(o)
-            arrive(rig.at[n, k], ri_s.at[o, k], ri_in.at[n, k])
+            arrive(rig.at[n, k], ri_s.at[o, k], ri_in.at[n, k], inside if k == moved else None)
+
+    def cross_of(block, k):
+        total = None
+        for b in range(C):
+            term = mm(block(b), lig[b, k])
+            total = term if total is None else total + term
+        return total.astype(BF16)
+
+    if moved < K:
+        for o in range(1, R):
+            n = row_peer(o)
+            arrive(ext.at[n], ext_s.at[o], ext_in.at[n], helper)
+
+        @pl.when(helper)
+        def _():
+            xs[...] = cross_of(lambda b: ext[b], moved)
+
+        copy(xs, xr, x_s.at[0], x_s.at[1], (r, served, d), helper)
+
+        @pl.when(inside)
+        def _():
+            cx[...] = cross_of(lambda b: rig[b, moved], moved)
+
     for o in range(1, R):
         n = row_peer(o)
         arrive(probe.at[n], pr_s.at[o], pr_in.at[n])
@@ -181,11 +221,16 @@
     for k in range(K):
         if C > 2:
             forward_li(C - 1, k)
-        cross = None
-        for b in range(C):
-            term = mm(rig[b, k], lig[b, k])
-            cross = term if cross is None else cross + term
-        cross = cross.astype(BF16)
+        if k == moved:
+            arrive(xr, x_s.at[0], x_s.at[1], at_end)
+
+            @pl.when(at_end)
+            def _():
+                cx[...] = xr[...]
+
+            cross = cx[...]
+        else:
+            cross = cross_of(lambda b: rig[b, k], k)
         weight = mask[0, 0, k].astype(F32) * scale
         right = (mm(probe[k // KR, k % KR], cross) * weight).astype(BF16)
         lanes = pl.ds(k * rank, rank)
@@ -337,12 +382,17 @@
         vmem((D, R, BR // D, rank), F32),
         vmem((R, BR // D, rank), BF16),
         vmem((R, BR // D, rank), BF16),
+        vmem((R, rank, BR), BF16),
+        vmem((rank, rank), BF16),
+        vmem((rank, rank), BF16),
+        vmem((rank, rank), BF16),
         dma((C, K)), dma((C, K)), dma((C, K)), dma((R, K)), dma((R, K)),
         dma((R,)), dma((R,)), dma((R,)), dma((R,)),
         dma((C,)), dma((C,)), dma((C,)), dma((C,)),
         dma((C, K)), dma((C, K)), dma((D,)), dma((D,)), dma((R, K)), dma((R, K)),
         dma((D, C)), dma((D, C)), dma((C,)), dma((C,)),
         dma((D, R)), dma((D, R)), dma((R,)), dma((R,)),
+        dma((R,)), dma((R,)), dma((2,)),
     ]
     tile = BL * C
     whole = pl.BlockSpec(memory_space=pltpu.VMEM)

time: 86.2 us -> 74.7 us (0.87)
  Pallas kernels: 83.4 us -> 71.8 us
    pallas_call x1, Pallas kernels: 83.4 us -> 71.8 us  [body(): pl.pallas_call(functools.partial(kernel, (R, C, D, K)), out_shape=(out, o...]
where the time goes in v3:
time: 74.7 us; the launch traced here: 74.5 us
  Pallas kernels  71.8 us (96%)
  other arithmetic  2.07 us (3%)
    pallas_call x1, Pallas kernels, body(): pl.pallas_call(functools.partial(kernel, (R, C, D, K)), out_shape=(out, o...  71.8 us
    convert_element_type x1, other arithmetic, body(): corange_rows[None, None].astype(F32)  2.07 us

profile of v3, /device:TPU:0, one launch (start us, length us, event | category | flops | bytes accessed | tf_op | source)
XLA Modules:
  0.0 74.5 jit_solution(7130976363075856530)
XLA Ops:
  0.6 71.8 %shard_map.86 = (bf16[1024,128]{1,0:T(8,128)(2,1)}, bf16[1024,128]{1,0:T(8,128)(2,1)}) custom-call(bf16[4,512,128]{2,1,0:T(8,128)(2,1)} %bitcast.12, bf16[4,512,128]{2,1,0:T(8,128)(2,1)} %bitcast.13, bf16[4,512,128]{2,1,0:T(8,128)(2,1)} %bitcast.14, bf16[4,512,128]{2,1,0:T(8,128)(2,1)} %bitcast.15, bf16[512,128]{1,0:T(8,128)(2,1)} %bitcast.17, ...), custom_call_target="tpu_custom_call" | custom-call | tf_op jit(solution)/shard_map/pallas_call | solution.py:400
  72.5 2.1 %bitcast_convert_fusion = (f32[1,1,1024,128]{3,2,1,0:T(8,128)}, f32[1,1,1024,128]{3,2,1,0:T(8,128)}) fusion(bf16[1024,128]{1,0:T(8,128)(2,1)} %get-tuple-element.5, bf16[1024,128]{1,0:T(8,128)(2,1)} %get-tuple-element.4), kind=kLoop, calls=%fused_computation | loop fusion | flops 262144 | bytes 1572864 | tf_op jit(solution)/shard_map/convert_element_type | solution.py:411

commit v4 on v3

--- a/solution.py
+++ b/solution.py
@@ -135,7 +135,7 @@
 
     ct_rows = ct[...].T
     for k in range(K):
-        tp[k] = mm(ct_rows, lo[k])
+        tp[k] = mm(ct_rows, lo[k]).astype(BF16)
     for o in range(1, C):
         n = col_peer(o)
         copy(tp.at[pl.ds(n * KC, KC)], tpr.at[c], tp_s.at[o], tp_in.at[c], (r, n, d))
@@ -160,11 +160,11 @@
         for o in range(1, R):
             copy(ext.at[r], ext.at[r], ext_s.at[o], ext_in.at[r], (row_peer(o), c, d), helper)
 
-    total = tp[pl.ds(c * KC, KC)]
+    total = tp[pl.ds(c * KC, KC)].astype(F32)
     for o in range(1, C):
         n = col_peer(o)
         arrive(tpr.at[n], tp_s.at[o], tp_in.at[n])
-        total = total + tpr[n]
+        total = total + tpr[n].astype(F32)
     test[c] = total.astype(BF16)
     for o in range(1, C):
         copy(test.at[c], test.at[c], te_s.at[o], te_in.at[c], (r, col_peer(o), d))
@@ -367,8 +367,8 @@
         vmem((K, rank, rank), F32),
         vmem((R, KR, rank, rank), F32),
         vmem((R, KR, rank, rank), BF16),
-        vmem((K, sketch, rank), F32),
-        vmem((C, KC, sketch, rank), F32),
+        vmem((K, sketch, rank), BF16),
+        vmem((C, KC, sketch, rank), BF16),
         vmem((C, KC, sketch, rank), BF16),
         vmem((C, rank, K * rank), BF16),
         vmem((rank, sketch), F32),

time: 74.7 us -> 70.6 us (0.945)
  Pallas kernels: 71.8 us -> 67.8 us
    pallas_call x1, Pallas kernels: 71.8 us -> 67.8 us  [body(): pl.pallas_call(functools.partial(kernel, (R, C, D, K)), out_shape=(out, o...]
where the time goes in v4:
time: 70.6 us; the launch traced here: 70.5 us
  Pallas kernels  67.8 us (96%)
  other arithmetic  2.07 us (3%)
    pallas_call x1, Pallas kernels, body(): pl.pallas_call(functools.partial(kernel, (R, C, D, K)), out_shape=(out, o...  67.8 us
    convert_element_type x1, other arithmetic, body(): corange_rows[None, None].astype(F32)  2.07 us

profile of v4, /device:TPU:0, one launch (start us, length us, event | category | flops | bytes accessed | tf_op | source)
XLA Modules:
  0.0 70.5 jit_solution(8221352690905204683)
XLA Ops:
  0.6 67.8 %shard_map.86 = (bf16[1024,128]{1,0:T(8,128)(2,1)}, bf16[1024,128]{1,0:T(8,128)(2,1)}) custom-call(bf16[4,512,128]{2,1,0:T(8,128)(2,1)} %bitcast.12, bf16[4,512,128]{2,1,0:T(8,128)(2,1)} %bitcast.13, bf16[4,512,128]{2,1,0:T(8,128)(2,1)} %bitcast.14, bf16[4,512,128]{2,1,0:T(8,128)(2,1)} %bitcast.15, bf16[512,128]{1,0:T(8,128)(2,1)} %bitcast.17, ...), custom_call_target="tpu_custom_call" | custom-call | tf_op jit(solution)/shard_map/pallas_call | solution.py:400
  68.4 2.1 %bitcast_convert_fusion = (f32[1,1,1024,128]{3,2,1,0:T(8,128)}, f32[1,1,1024,128]{3,2,1,0:T(8,128)}) fusion(bf16[1024,128]{1,0:T(8,128)(2,1)} %get-tuple-element.5, bf16[1024,128]{1,0:T(8,128)(2,1)} %get-tuple-element.4), kind=kLoop, calls=%fused_computation | loop fusion | flops 262144 | bytes 1572864 | tf_op jit(solution)/shard_map/convert_element_type | solution.py:411
